TPU v7x, 256 devices: a whole 4x4x8 slice. The times are simulated.
256 devices in a mesh: row: 32 (over y, x, z_hi), col: 8 (over z_lo, core).
Axes of the slice: x: 4, y: 4, z: 8 (z_hi: 2, z_lo: 4; z = z_hi * 4 + z_lo), core: 2. Of those that a mesh axis runs over, the one named last changes fastest.
Arguments:
- hamiltonian_blocks: bfloat16 [32, 8, 64, 128, 128], P('row', 'col'), may hold values from -0.046875 to 0.046875
- block_rows: int32 [32, 8, 64], P('row', 'col'), may hold values from 0 to 7, as said below
- block_cols: int32 [32, 8, 64], P('row', 'col'), may hold values from 0 to 31
- block_counts: int32 [32, 8], P('row', 'col'), may hold values from 16 to 64, as said below
- initial: float32 [32768, 128], P(('row', 'col')), may hold values from -6 to 6
- center: float32 [1], replicated, may hold values from -0.3 to 0.3
- halfwidth: float32 [1], replicated, may hold values from 1 to 1.5
Outputs:
- filtered: float32 [32768, 128], P(('row', 'col'))
Inputs may be any that keep to these rules, and one draw needn't show every extreme that they name: `block_rows`: padded slots hold arbitrary values. `block_counts`: some tile is full in every draw.
All inputs are finite; a program needn't handle non-finite values.
Results may differ from a plain program's by a relative error of at most 0.0068.
Values may be sent and summed in bfloat16 or wider, within the bound.
A program may use at most 128 MiB of HBM per device.

v0:
```python
import jax
import jax.numpy as jnp
from jax import lax
from jax.sharding import PartitionSpec as P

SLAB = 1
DEGREE = 3


def body(hamiltonian_blocks, block_rows, block_cols, block_counts, initial, center, halfwidth):
    stacked = hamiltonian_blocks[0, 0]
    slot_rows = block_rows[0, 0]
    slot_cols = block_cols[0, 0]
    live_count = block_counts[0, 0]
    grid_rows = lax.axis_size("row")
    grid_cols = lax.axis_size("col")
    orbitals = stacked.shape[1]
    vectors = initial.shape[1]
    slots = stacked.shape[0]
    row_segments = grid_cols * SLAB
    col_segments = grid_rows * SLAB
    highest = lax.Precision.HIGHEST
    is_live = jnp.arange(slots, dtype=jnp.int32) < live_count
    row_onehot = (
        (slot_rows[None, :] == jnp.arange(row_segments, dtype=jnp.int32)[:, None])
        & is_live[None, :]
    ).astype(jnp.float32)
    col_onehot = (
        (slot_cols[None, :] == jnp.arange(col_segments, dtype=jnp.int32)[:, None])
        & is_live[None, :]
    ).astype(jnp.float32)
    previous = initial
    current = initial
    for degree_step in range(DEGREE):
        panel = current.astype(jnp.bfloat16)
        apply_column_panel = lax.all_gather(panel, "row", axis=0, tiled=True).reshape(
            -1, orbitals, vectors
        )
        apply_row_panel = lax.all_gather(panel, "col", axis=0, tiled=True).reshape(
            -1, orbitals, vectors
        )
        upper_products = jnp.einsum(
            "sab,sbv->sav",
            stacked,
            apply_column_panel[slot_cols],
            preferred_element_type=jnp.float32,
        )
        upper_partial = jnp.einsum("ts,sav->tav", row_onehot, upper_products, precision=highest)
        upper_sum = lax.psum_scatter(
            upper_partial.reshape(-1, vectors), "col", scatter_dimension=0, tiled=True
        )
        products = jnp.einsum(
            "sba,sbv->sav", stacked, apply_row_panel[slot_rows], preferred_element_type=jnp.float32
        )
        lower_partial = jnp.einsum("ts,sav->tav", col_onehot, products, precision=highest)
        lower_sum = lax.psum_scatter(
            lower_partial.reshape(-1, vectors), "row", scatter_dimension=0, tiled=True
        )
        applied = upper_sum + lower_sum
        shifted = (applied - center[0] * current) / halfwidth[0]
        if degree_step == 0:
            following = shifted
        else:
            following = 2.0 * shifted - previous
        previous = current
        current = following
    return current


def solution(mesh):
    in_specs = (
        P("row", "col", None, None, None),
        P("row", "col", None),
        P("row", "col", None),
        P("row", "col"),
        P(("row", "col"), None),
        P(),
        P(),
    )
    out_specs = P(("row", "col"), None)
    return jax.shard_map(body, mesh=mesh, in_specs=in_specs, out_specs=out_specs, check_vma=False)
```

profile of v0, /device:TPU:32, one launch (start us, length us, event | category | flops | bytes accessed | tf_op | source)
XLA Modules:
  0.0 1112.5 jit_solution(9385953845992300890)
XLA Ops:
  6.5 1.6 convert_element_type.11
  8.1 0.0 all-gather.4.cloned.1.call-update
  8.2 0.0 reduce-scatter.7.cloned.1.call-start
  8.9 0.7 fusion.46
  9.6 83.8 %all-gather.4.cloned.1.call-done = bf16[4096,128]{1,0:T(8,128)(2,1)} async-done(((bf16[128,128]{1,0:T(8,128)(2,1)}), bf16[4096,128]{1,0:T(8,128)(2,1)}) %all-gather.4.cloned.1.call-update) | async-done | bytes 1048592 | tf_op jit(solution)/shard_map/all_gather | solution.py:36
  93.4 3.4 gather_fusion
  96.8 5.2 fusion.22
  102.0 5.4 copy.14
  107.4 3.7 fusion.10
  111.1 0.9 copy.8
  112.0 0.0 reduce-scatter.7.cloned.1.call-update
  112.0 0.0 reduce-scatter.9.cloned.1.call-start
  112.1 13.5 %all_gather.19 = bf16[1024,128]{1,0:T(8,128)(2,1)S(1)} all-gather(bf16[128,128]{1,0:T(8,128)(2,1)S(1)} %copy-done.2), channel_id=1, replica_groups=mesh['row'=32,'col'=8] {'col'}, dimensions={0}, use_global_device_ids=true | all-gather | bytes 294912 | tf_op jit(solution)/shard_map/all_gather | solution.py:39
  125.6 2.2 gather_fusion.1
  127.8 4.4 fusion.20
  132.2 5.4 copy.15
  137.6 4.0 fusion.8
  141.7 2.6 copy.9
  144.2 0.0 reduce-scatter.9.cloned.1.call-update
  144.2 0.0 all-gather.6.cloned.1.call-start
  145.6 0.0 reduce-scatter.7.cloned.1.call-done
  145.6 234.6 %reduce-scatter.9.cloned.1.call-done = f32[128,128]{1,0:T(8,128)} async-done(((f32[4096,128]{1,0:T(8,128)}), f32[128,128]{1,0:T(8,128)}) %reduce-scatter.9.cloned.1.call-update) | async-done | bytes 65552 | tf_op jit(solution)/shard_map/reduce_scatter | solution.py:56
  380.3 1.5 fusion.49
  381.8 0.0 all-gather.6.cloned.1.call-update
  381.8 0.2 reduce-scatter.11.cloned.1.call-start
  382.0 73.9 %all-gather.6.cloned.1.call-done = bf16[4096,128]{1,0:T(8,128)(2,1)} async-done(((bf16[128,128]{1,0:T(8,128)(2,1)}), bf16[4096,128]{1,0:T(8,128)(2,1)}) %all-gather.6.cloned.1.call-update) | async-done | bytes 1048592 | tf_op jit(solution)/shard_map/all_gather | solution.py:36
  455.9 3.4 gather_fusion.2
  459.3 5.2 fusion.18
  464.5 5.4 copy.16
  469.9 3.7 fusion.6
  473.5 0.9 copy.10
  474.5 0.0 reduce-scatter.11.cloned.1.call-update
  474.5 0.0 reduce-scatter.13.cloned.1.call-start
  474.6 13.5 %all_gather.21 = bf16[1024,128]{1,0:T(8,128)(2,1)S(1)} all-gather(bf16[128,128]{1,0:T(8,128)(2,1)S(1)} %copy-done.3), channel_id=1, replica_groups=mesh['row'=32,'col'=8] {'col'}, dimensions={0}, use_global_device_ids=true | all-gather | bytes 294912 | tf_op jit(solution)/shard_map/all_gather | solution.py:39
  488.0 2.2 gather_fusion.3
  490.2 4.4 fusion.16
  494.6 5.4 copy.17
  500.1 4.0 fusion.4
  504.1 2.6 copy.11
  506.7 0.0 reduce-scatter.13.cloned.1.call-update
  506.7 0.0 all-gather.8.cloned.1.call-start
  506.7 0.0 reduce-scatter.11.cloned.1.call-done
  506.8 235.0 %reduce-scatter.13.cloned.1.call-done = f32[128,128]{1,0:T(8,128)} async-done(((f32[4096,128]{1,0:T(8,128)}), f32[128,128]{1,0:T(8,128)}) %reduce-scatter.13.cloned.1.call-update) | async-done | bytes 65552 | tf_op jit(solution)/shard_map/reduce_scatter | solution.py:56
  741.7 1.5 fusion.48
  743.2 0.0 all-gather.8.cloned.1.call-update
  743.2 0.3 reduce-scatter.15.cloned.1.call-start
  743.5 74.6 %all-gather.8.cloned.1.call-done = bf16[4096,128]{1,0:T(8,128)(2,1)} async-done(((bf16[128,128]{1,0:T(8,128)(2,1)}), bf16[4096,128]{1,0:T(8,128)(2,1)}) %all-gather.8.cloned.1.call-update) | async-done | bytes 1048592 | tf_op jit(solution)/shard_map/all_gather | solution.py:36
  818.1 3.4 gather_fusion.4
  821.5 5.2 fusion.14
  826.7 5.4 copy.18
  832.1 3.7 fusion.2
  835.7 0.9 copy.12
  836.7 0.0 reduce-scatter.15.cloned.1.call-update
  836.7 0.0 reduce-scatter.17.cloned.1.call-start
  836.8 13.5 %all_gather.23 = bf16[1024,128]{1,0:T(8,128)(2,1)S(1)} all-gather(bf16[128,128]{1,0:T(8,128)(2,1)S(1)} %copy-done.4), channel_id=1, replica_groups=mesh['row'=32,'col'=8] {'col'}, dimensions={0}, use_global_device_ids=true | all-gather | bytes 294912 | tf_op jit(solution)/shard_map/all_gather | solution.py:39
  850.2 2.2 gather_fusion.5
  852.4 4.4 fusion.12
  856.8 5.4 copy.19
  862.3 4.0 fusion
  866.3 2.6 copy.13
  868.9 0.0 reduce-scatter.17.cloned.1.call-update
  868.9 0.0 reduce-scatter.15.cloned.1.call-done
  868.9 235.5 %reduce-scatter.17.cloned.1.call-done = f32[128,128]{1,0:T(8,128)} async-done(((f32[4096,128]{1,0:T(8,128)}), f32[128,128]{1,0:T(8,128)}) %reduce-scatter.17.cloned.1.call-update) | async-done | bytes 65552 | tf_op jit(solution)/shard_map/reduce_scatter | solution.py:56
  1104.5 1.5 multiply_subtract_fusion
  (19 shorter events, 0.1 us)
Async XLA Ops:
  6.5 90.3 %copy-start = (bf16[1,1,64,128,128]{4,3,2,1,0:T(8,128)(2,1)S(1)}, bf16[1,1,64,128,128]{4,3,2,1,0:T(8,128)(2,1)}, u32[]{:S(2)}) copy-start(bf16[1,1,64,128,128]{4,3,2,1,0:T(8,128)(2,1)} %param.7) | copy-start | bytes 6291460
  6.5 86.9 %all-gather.4.cloned.1.call-start = ((), (), s32[]{:S(2)}) async-start(), calls=%async_computation.6 | async-start | bytes 1081344 | tf_op jit(solution)/shard_map/all_gather | solution.py:36
  8.2 137.4 %reduce-scatter.7.cloned.1.call-start = ((), (), s32[]{:S(2)}) async-start(), calls=%async_computation.7 | async-start | bytes 589824 | tf_op jit(solution)/shard_map/reduce_scatter | solution.py:49
  102.0 5.4 copy-start.5
  107.4 4.7 copy-start.2
  112.0 268.2 %reduce-scatter.9.cloned.1.call-start = ((), (), s32[]{:S(2)}) async-start(), calls=%async_computation.8 | async-start | bytes 2162688 | tf_op jit(solution)/shard_map/reduce_scatter | solution.py:56
  132.2 5.4 copy-start.6
  144.2 236.0 %copy-start.1 = (f32[128,128]{1,0:T(8,128)S(1)}, f32[128,128]{1,0:T(8,128)}, u32[]{:S(2)}) copy-start(f32[128,128]{1,0:T(8,128)} %param.11) | copy-start | bytes 196612
  144.2 311.7 %all-gather.6.cloned.1.call-start = ((), (), s32[]{:S(2)}) async-start(), calls=%async_computation.9 | async-start | bytes 1081344 | tf_op jit(solution)/shard_map/all_gather | solution.py:36
  381.8 125.0 %reduce-scatter.11.cloned.1.call-start = ((), (), s32[]{:S(2)}) async-start(), calls=%async_computation.10 | async-start | bytes 589824 | tf_op jit(solution)/shard_map/reduce_scatter | solution.py:49
  469.9 4.7 copy-start.3
  474.5 267.2 %reduce-scatter.13.cloned.1.call-start = ((), (), s32[]{:S(2)}) async-start(), calls=%async_computation.11 | async-start | bytes 2162688 | tf_op jit(solution)/shard_map/reduce_scatter | solution.py:56
  506.7 311.4 %all-gather.8.cloned.1.call-start = ((), (), s32[]{:S(2)}) async-start(), calls=%async_computation.12 | async-start | bytes 1081344 | tf_op jit(solution)/shard_map/all_gather | solution.py:36
  743.2 125.7 %reduce-scatter.15.cloned.1.call-start = ((), (), s32[]{:S(2)}) async-start(), calls=%async_computation.13 | async-start | bytes 589824 | tf_op jit(solution)/shard_map/reduce_scatter | solution.py:49
  832.1 4.7 copy-start.4
  836.7 267.8 %reduce-scatter.17.cloned.1.call-start = ((), (), s32[]{:S(2)}) async-start(), calls=%async_computation.14 | async-start | bytes 2162688 | tf_op jit(solution)/shard_map/reduce_scatter | solution.py:56
Sparse Core Ops, SparseCore 0:
  10.7 82.6 all-gather.3
  112.1 28.7 reduce-scatter.6
  144.4 235.8 reduce-scatter.8
  383.5 72.3 all-gather.5
  474.6 28.6 reduce-scatter.10
  506.8 234.8 reduce-scatter.12
  745.1 72.9 all-gather.7
  836.8 28.6 reduce-scatter.14
  869.0 235.3 reduce-scatter.16
where the time goes:
time: 1110 us
  waiting for transfers between devices  938 us (85%)
  local copies, waits for them, and re-layouts  59.8 us (5%)
  matrix products  51.8 us (5%)
  blocking collectives  40.5 us (4%)
  between operations  15.3 us (1%)
    reduce_scatter x3, waiting for transfers between devices, body(): lax.psum_scatter(lower_partial.reshape(-1, vectors), 'row', scatter_dimen...  705 us
    all_gather x3, waiting for transfers between devices, body(): lax.all_gather(panel, 'row', axis=0, tiled=True)  232 us
    all_gather x3, blocking collectives, body(): lax.all_gather(panel, 'col', axis=0, tiled=True)  40.5 us
  transfers between devices with their start and end apart: 9, of which 6 were waited for; matrix products, arithmetic and copies ran while one was open for 5% of the time, Pallas kernels for 0%

commit v1 on v0

--- a/solution.py
+++ b/solution.py
@@ -33,9 +33,9 @@
     current = initial
     for degree_step in range(DEGREE):
         panel = current.astype(jnp.bfloat16)
-        apply_column_panel = lax.all_gather(panel, "row", axis=0, tiled=True).reshape(
-            -1, orbitals, vectors
-        )
+        apply_column_panel = jnp.concatenate(
+            lax.all_to_all(jnp.stack([panel] * lax.axis_size("row")), "row", 0, 0), axis=0
+        ).reshape(-1, orbitals, vectors)
         apply_row_panel = lax.all_gather(panel, "col", axis=0, tiled=True).reshape(
             -1, orbitals, vectors
         )

time: 1110 us -> 977 us (0.88)
  waiting for transfers between devices: 938 us -> 743 us
  blocking collectives: 40.5 us -> 90.6 us
  starting transfers between devices: 0.74 us -> 13.3 us
    all_gather x3 -> x0, waiting for transfers between devices: 232 us -> none  [body(): lax.all_gather(panel, 'row', axis=0, tiled=True)]
    all_to_all x0 -> x2, blocking collectives: none -> 52.4 us  [body(): lax.all_to_all(jnp.stack([panel] * lax.axis_size('row')), 'row', 0, 0)]
    all_to_all x0 -> x1, waiting for transfers between devices: none -> 32.2 us  [body(): lax.all_to_all(jnp.stack([panel] * lax.axis_size('row')), 'row', 0, 0)]
    all_to_all x0 -> x1, starting transfers between devices: none -> 13 us  [body(): lax.all_to_all(jnp.stack([panel] * lax.axis_size('row')), 'row', 0, 0)]
  transfers between devices with their start and end apart: 9 -> 7, of which waited for: 6 -> 4; matrix products, arithmetic and copies ran while one was open for 5% -> 6% of each run, Pallas kernels for 0% -> 0%
where the time goes in v1:
time: 977 us; the launch traced here: 976 us
  waiting for transfers between devices  743 us (76%)
  blocking collectives  90.6 us (9%)
  local copies, waits for them, and re-layouts  57.4 us (6%)
  matrix products  51.7 us (5%)
  between operations  15.6 us (2%)
  starting transfers between devices  13.3 us (1%)
    reduce_scatter x3, waiting for transfers between devices, body(): lax.psum_scatter(lower_partial.reshape(-1, vectors), 'row', scatter_dimen...  711 us
    all_to_all x2, blocking collectives, body(): lax.all_to_all(jnp.stack([panel] * lax.axis_size('row')), 'row', 0, 0)  52.4 us
    all_gather x3, blocking collectives, body(): lax.all_gather(panel, 'col', axis=0, tiled=True)  38.2 us
    all_to_all x1, waiting for transfers between devices, body(): lax.all_to_all(jnp.stack([panel] * lax.axis_size('row')), 'row', 0, 0)  32.2 us
  transfers between devices with their start and end apart: 7, of which 4 were waited for; matrix products, arithmetic and copies ran while one was open for 6% of the time, Pallas kernels for 0%

profile of v1, /device:TPU:32, one launch (start us, length us, event | category | flops | bytes accessed | tf_op | source)
XLA Modules:
  0.0 975.8 jit_solution(2471129629645405920)
XLA Ops:
  6.5 0.0 copy-start
  6.5 1.0 convert_element_type.11
  7.5 1.2 stack.6
  8.8 13.0 %all-to-all-start = ((bf16[32,128,128]{2,1,0:T(8,128)(2,1)}), bf16[32,128,128]{2,1,0:T(8,128)(2,1)S(1)}, u32[]{:S(2)}, u32[]{:S(2)}) async-start(bf16[32,128,128]{2,1,0:T(8,128)(2,1)} %stack.6), calls=%async_computation | async-start | bytes 2097152 | tf_op jit(solution)/shard_map/all_to_all | solution.py:37
  21.8 0.0 reduce-scatter.7.cloned.1.call-start
  22.5 0.0 copy-done.3
  22.5 32.2 %all-to-all-done = bf16[32,128,128]{2,1,0:T(8,128)(2,1)S(1)} async-done(((bf16[32,128,128]{2,1,0:T(8,128)(2,1)}), bf16[32,128,128]{2,1,0:T(8,128)(2,1)S(1)}, u32[]{:S(2)}, u32[]{:S(2)}) %all-to-all-start) | async-done | bytes 1048608 | tf_op jit(solution)/shard_map/all_to_all | solution.py:37
  54.8 2.1 gather_fusion
  56.9 5.1 fusion.22
  62.1 5.4 copy.14
  67.5 3.7 fusion.10
  71.1 0.9 copy.8
  72.1 0.0 reduce-scatter.7.cloned.1.call-update
  72.1 0.0 reduce-scatter.9.cloned.1.call-start
  72.2 13.0 %all_gather.9 = bf16[1024,128]{1,0:T(8,128)(2,1)S(1)} all-gather(bf16[128,128]{1,0:T(8,128)(2,1)S(1)} %convert_element_type.11), channel_id=1, replica_groups=mesh['row'=32,'col'=8] {'col'}, dimensions={0}, use_global_device_ids=true | all-gather | bytes 294912 | tf_op jit(solution)/shard_map/all_gather | solution.py:39
  85.1 2.1 gather_fusion.1
  87.3 4.4 fusion.20
  91.7 5.4 copy.15
  97.1 4.0 fusion.8
  101.2 2.6 copy.9
  103.7 0.0 reduce-scatter.9.cloned.1.call-update
  103.7 0.0 reduce-scatter.11.cloned.1.call-start
  105.1 0.0 reduce-scatter.7.cloned.1.call-done
  105.1 236.5 %reduce-scatter.9.cloned.1.call-done = f32[128,128]{1,0:T(8,128)} async-done(((f32[4096,128]{1,0:T(8,128)}), f32[128,128]{1,0:T(8,128)}) %reduce-scatter.9.cloned.1.call-update) | async-done | bytes 65552 | tf_op jit(solution)/shard_map/reduce_scatter | solution.py:56
  341.6 0.9 fusion.49
  342.5 0.2 stack.7
  342.7 26.2 %all_to_all.15 = bf16[32,128,128]{2,1,0:T(8,128)(2,1)S(1)} all-to-all(bf16[32,128,128]{2,1,0:T(8,128)(2,1)S(1)} %stack.7), channel_id=1, replica_groups=mesh['row'=32,'col'=8] {'row'}, dimensions={0} | all-to-all | bytes 2097152 | tf_op jit(solution)/shard_map/all_to_all | solution.py:37
  368.9 2.1 gather_fusion.2
  371.1 5.1 fusion.18
  376.2 5.4 copy.16
  381.6 3.7 fusion.6
  385.2 0.9 copy.10
  386.2 0.0 reduce-scatter.11.cloned.1.call-update
  386.2 0.0 reduce-scatter.13.cloned.1.call-start
  386.2 12.5 %all_gather.10 = bf16[1024,128]{1,0:T(8,128)(2,1)S(1)} all-gather(bf16[128,128]{1,0:T(8,128)(2,1)S(1)} %get-tuple-element.7), channel_id=1, replica_groups=mesh['row'=32,'col'=8] {'col'}, dimensions={0}, use_global_device_ids=true | all-gather | bytes 294912 | tf_op jit(solution)/shard_map/all_gather | solution.py:39
  398.8 2.1 gather_fusion.3
  400.9 4.4 fusion.16
  405.3 5.4 copy.17
  410.7 4.0 fusion.4
  414.7 2.6 copy.11
  417.3 0.0 reduce-scatter.13.cloned.1.call-update
  417.3 0.0 reduce-scatter.15.cloned.1.call-start
  417.4 0.0 reduce-scatter.11.cloned.1.call-done
  417.4 239.8 %reduce-scatter.13.cloned.1.call-done = f32[128,128]{1,0:T(8,128)} async-done(((f32[4096,128]{1,0:T(8,128)}), f32[128,128]{1,0:T(8,128)}) %reduce-scatter.13.cloned.1.call-update) | async-done | bytes 65552 | tf_op jit(solution)/shard_map/reduce_scatter | solution.py:56
  657.2 0.9 fusion.48
  658.1 0.2 stack.8
  658.4 26.2 %all_to_all.16 = bf16[32,128,128]{2,1,0:T(8,128)(2,1)S(1)} all-to-all(bf16[32,128,128]{2,1,0:T(8,128)(2,1)S(1)} %stack.8), channel_id=1, replica_groups=mesh['row'=32,'col'=8] {'row'}, dimensions={0} | all-to-all | bytes 2097152 | tf_op jit(solution)/shard_map/all_to_all | solution.py:37
  684.6 2.1 gather_fusion.4
  686.7 5.1 fusion.14
  691.8 5.4 copy.18
  697.2 3.7 fusion.2
  700.9 0.9 copy.12
  701.8 0.0 reduce-scatter.15.cloned.1.call-update
  701.8 0.0 reduce-scatter.17.cloned.1.call-start
  701.9 12.7 %all_gather.11 = bf16[1024,128]{1,0:T(8,128)(2,1)S(1)} all-gather(bf16[128,128]{1,0:T(8,128)(2,1)S(1)} %get-tuple-element.5), channel_id=1, replica_groups=mesh['row'=32,'col'=8] {'col'}, dimensions={0}, use_global_device_ids=true | all-gather | bytes 294912 | tf_op jit(solution)/shard_map/all_gather | solution.py:39
  714.6 2.1 gather_fusion.5
  716.7 4.4 fusion.12
  721.1 5.4 copy.19
  726.5 4.0 fusion
  730.6 2.6 copy.13
  733.2 0.0 reduce-scatter.17.cloned.1.call-update
  733.2 0.0 reduce-scatter.15.cloned.1.call-done
  733.2 234.2 %reduce-scatter.17.cloned.1.call-done = f32[128,128]{1,0:T(8,128)} async-done(((f32[4096,128]{1,0:T(8,128)}), f32[128,128]{1,0:T(8,128)}) %reduce-scatter.17.cloned.1.call-update) | async-done | bytes 65552 | tf_op jit(solution)/shard_map/reduce_scatter | solution.py:56
  967.4 1.5 multiply_subtract_fusion
  (11 shorter events, 0.0 us)
Async XLA Ops:
  6.5 50.4 %copy-start = (bf16[1,1,64,128,128]{4,3,2,1,0:T(8,128)(2,1)S(1)}, bf16[1,1,64,128,128]{4,3,2,1,0:T(8,128)(2,1)}, u32[]{:S(2)}) copy-start(bf16[1,1,64,128,128]{4,3,2,1,0:T(8,128)(2,1)} %param.7) | copy-start | bytes 6291460
  6.5 16.0 %copy-start.3 = (s32[1,1,64]{2,1,0:T(1,128)S(1)}, s32[1,1,64]{2,1,0:T(1,128)}, u32[]{:S(2)}) copy-start(s32[1,1,64]{2,1,0:T(1,128)} %param.9) | copy-start | bytes 772
  8.8 46.0 %all-to-all-start = ((bf16[32,128,128]{2,1,0:T(8,128)(2,1)}), bf16[32,128,128]{2,1,0:T(8,128)(2,1)S(1)}, u32[]{:S(2)}, u32[]{:S(2)}) async-start(bf16[32,128,128]{2,1,0:T(8,128)(2,1)} %stack.6), calls=%async_computation | async-start | bytes 2097152 | tf_op jit(solution)/shard_map/all_to_all | solution.py:37
  21.8 83.3 %reduce-scatter.7.cloned.1.call-start = ((), (), s32[]{:S(2)}) async-start(), calls=%async_computation.9 | async-start | bytes 589824 | tf_op jit(solution)/shard_map/reduce_scatter | solution.py:49
  62.1 5.4 copy-start.2
  72.1 269.5 %reduce-scatter.9.cloned.1.call-start = ((), (), s32[]{:S(2)}) async-start(), calls=%async_computation.10 | async-start | bytes 2162688 | tf_op jit(solution)/shard_map/reduce_scatter | solution.py:56
  103.7 237.9 %copy-start.1 = (f32[128,128]{1,0:T(8,128)S(1)}, f32[128,128]{1,0:T(8,128)}, u32[]{:S(2)}) copy-start(f32[128,128]{1,0:T(8,128)} %param.11) | copy-start | bytes 196612
  103.7 313.7 %reduce-scatter.11.cloned.1.call-start = ((), (), s32[]{:S(2)}) async-start(), calls=%async_computation.11 | async-start | bytes 589824 | tf_op jit(solution)/shard_map/reduce_scatter | solution.py:49
  386.2 271.0 %reduce-scatter.13.cloned.1.call-start = ((), (), s32[]{:S(2)}) async-start(), calls=%async_computation.12 | async-start | bytes 2162688 | tf_op jit(solution)/shard_map/reduce_scatter | solution.py:56
  417.3 315.9 %reduce-scatter.15.cloned.1.call-start = ((), (), s32[]{:S(2)}) async-start(), calls=%async_computation.13 | async-start | bytes 589824 | tf_op jit(solution)/shard_map/reduce_scatter | solution.py:49
  701.8 265.6 %reduce-scatter.17.cloned.1.call-start = ((), (), s32[]{:S(2)}) async-start(), calls=%async_computation.14 | async-start | bytes 2162688 | tf_op jit(solution)/shard_map/reduce_scatter | solution.py:56
Sparse Core Ops, SparseCore 0:
  72.2 27.0 reduce-scatter.6
  103.9 237.6 reduce-scatter.8
  386.3 27.6 reduce-scatter.10
  417.5 239.7 reduce-scatter.12
  701.9 26.6 reduce-scatter.14
  733.3 234.0 reduce-scatter.16
